TPU v7x, 32 devices: a whole 2x2x4 slice. The times are simulated.
32 devices in a mesh: groups: 2 (over y), wide: 4 (over z), narrow: 4 (over x, core).
Axes of the slice: x: 2, y: 2, z: 4, core: 2. Of those that a mesh axis runs over, the one named last changes fastest.
Arguments:
- hidden: bfloat16 [4096, 4096], P(('groups', 'wide')), parts along dimension 0, may hold values from -16 to 16
- w_qkv: bfloat16 [4096, 3, 2048], P('wide', None, 'narrow'), may hold values from -0.09375 to 0.09375
- w_out: bfloat16 [2048, 4096], P(None, 'wide'), may hold values from -0.125 to 0.125
- seg_ids: int32 [4096], P('groups'), parts along dimension 0, may hold values from 0 to 3, never falling along the last dimension, each value on 1 to 1024 neighbouring positions
- shift_heads: int32 [16], replicated, may hold values from 0 to 1, as said below
Outputs:
- layer_out: bfloat16 [4096, 4096], P(('groups', 'wide', 'narrow')), parts along dimension 0
There are 2 independent parts, one for each index of `groups`. A program takes and returns all parts, laid end to end along the dimension named above; an argument that names none is the same for every part. Nothing has to cross between parts.
Inputs may be any that keep to these rules, and one draw needn't show every extreme that they name: `shift_heads`: exactly half of the heads are marked with 1, the others with 0. `seg_ids`: never falls along the window; every number occurs on 1 to 1024 consecutive tokens, one on exactly that many.
All inputs are finite; a program needn't handle non-finite values.
Results may differ from a plain program's by a relative error of at most 0.012.
Values may be sent and summed in bfloat16 or wider, within the bound.
A program may use at most 128 MiB of HBM per device.

v0:
```python
import math

import jax
import jax.numpy as jnp
from jax import lax
from jax.sharding import PartitionSpec as P

HEAD_DIM = 128
GROUP = 512
SHIFT = 256


masked_out = -1e30


def from_behind(block, axis, distance):
    devices = range(lax.axis_size(axis))
    route = [((i - distance) % len(devices), i) for i in devices]
    return lax.ppermute(block, axis, route)


def attend(query_rows, key_rows, value_rows, allowed):
    scores = jnp.einsum(
        "ihd,jhd->hij", query_rows, key_rows, preferred_element_type=jnp.float32
    ) * (1.0 / math.sqrt(HEAD_DIM))
    scores = jnp.where(allowed, scores, masked_out)
    row_max = jnp.max(scores, axis=-1, keepdims=True)
    exponent = jnp.exp(scores - row_max)
    weights = (exponent / jnp.sum(exponent, axis=-1, keepdims=True)).astype(jnp.bfloat16)
    combined = jnp.einsum("hij,jhd->ihd", weights, value_rows, preferred_element_type=jnp.float32)
    return combined.astype(jnp.bfloat16).reshape(query_rows.shape[0], -1)


def per_device(hidden, w_qkv, w_out, seg_ids, shift_heads):
    tok_rows = hidden.shape[0]
    local_f = w_qkv.shape[2]
    heads_here = local_f // HEAD_DIM
    groups_here = tok_rows // GROUP
    narrow_idx = lax.axis_index("narrow")
    first_tok = lax.axis_index("wide") * tok_rows
    shifted = lax.dynamic_slice_in_dim(shift_heads, narrow_idx * heads_here, heads_here) > 0
    projected = jnp.einsum(
        "tr,rcf->tcf",
        hidden,
        lax.all_gather(w_qkv, "wide", axis=0, tiled=True),
        preferred_element_type=jnp.float32,
    ).astype(jnp.bfloat16)
    incoming = from_behind(projected[:SHIFT], "wide", -1)
    rolled = jnp.concatenate([projected[SHIFT:], incoming], 0)
    feature_flag = jnp.repeat(shifted, HEAD_DIM)
    moved_qkv = jnp.where(feature_flag[None, None, :], rolled, projected)
    doubled = jnp.concatenate([seg_ids, seg_ids[:SHIFT]], 0)
    seg_own = lax.dynamic_slice_in_dim(seg_ids, first_tok, tok_rows)
    seg_rolled = lax.dynamic_slice_in_dim(doubled, first_tok + SHIFT, tok_rows)
    seg_heads = jnp.where(shifted[:, None], seg_rolled[None, :], seg_own[None, :])
    blocks = moved_qkv.reshape(groups_here, GROUP, 3, heads_here, HEAD_DIM)
    block_segs = seg_heads.reshape(heads_here, groups_here, GROUP).transpose(1, 0, 2)
    positions = jnp.arange(GROUP, dtype=jnp.int32)
    causal = positions[:, None] >= positions[None, :]

    def one_group(inputs):
        block_qkv, block_seg = inputs
        allowed = causal[None] & (block_seg[:, :, None] == block_seg[:, None, :])
        return attend(block_qkv[:, 0], block_qkv[:, 1], block_qkv[:, 2], allowed)

    att_rolled = lax.map(one_group, (blocks, block_segs)).reshape(tok_rows, local_f)
    carried = from_behind(att_rolled[tok_rows - SHIFT :], "wide", 1)
    restored = jnp.concatenate([carried, att_rolled[: tok_rows - SHIFT]], 0)
    attended = jnp.where(feature_flag[None, :], restored, att_rolled)
    own_rows = lax.dynamic_slice_in_dim(w_out, narrow_idx * local_f, local_f, 0)
    partial_value = jnp.dot(
        attended,
        lax.all_gather(own_rows, "wide", axis=1, tiled=True),
        preferred_element_type=jnp.float32,
    )
    layer_out = lax.psum_scatter(
        partial_value.astype(jnp.bfloat16), "narrow", scatter_dimension=0, tiled=True
    )
    return layer_out


def solution(mesh):
    placed = (
        P(("groups", "wide"), None),
        P("wide", None, "narrow"),
        P(None, "wide"),
        P("groups"),
        P(),
    )
    return jax.shard_map(
        per_device,
        mesh=mesh,
        in_specs=placed,
        out_specs=P(("groups", "wide", "narrow"), None),
        check_vma=False,
    )
```

profile of v0, /device:TPU:0, one launch (start us, length us, event | category | flops | bytes accessed | tf_op | source)
XLA Modules:
  0.0 391.4 jit_solution(4442015113571459259)
XLA Ops:
  6.5 4.7 %copy.6 = bf16[1024,3,512]{0,2,1:T(8,128)(2,1)} copy(bf16[1024,3,512]{2,0,1:T(8,128)(2,1)} %param.6) | data formatting | bytes 6291456 | tf_op args[1]
  11.2 0.0 all-gather.3.cloned.1.call-update
  11.2 0.0 all-gather.5.cloned.1.call-start
  11.3 2.3 constant_dynamic-slice_fusion
  13.6 0.0 all-gather.5.cloned.1.call-update
  13.6 0.0 reduce-scatter.2.cloned.1.call-start
  13.7 218.6 %all-gather.3.cloned.1.call-done = bf16[4096,3,512]{0,2,1:T(8,128)(2,1)} async-done(((bf16[1024,3,512]{0,2,1:T(8,128)(2,1)}), bf16[4096,3,512]{0,2,1:T(8,128)(2,1)}) %all-gather.3.cloned.1.call-update) | async-done | bytes 12582928 | tf_op jit(solution)/shard_map/all_gather | solution.py:45
  232.3 10.9 %fusion.10 = bf16[512,3,512]{0,2,1:T(8,128)(2,1)S(1)} fusion(bf16[4096,3,512]{0,2,1:T(8,128)(2,1)} %all-gather.3.cloned.1.call-done, bf16[512,4096]{1,0:T(8,128)(2,1)} %param.5), kind=kOutput, calls=%fused_computation.14 | convolution fusion | flops 6443237376 | bytes 18350080 | tf_op jit(solution)/shard_map/tr,rcf->tcf/dot_general | solution.py:42
  243.2 0.1 fusion.29
  243.3 0.3 collective-permute-start
  243.7 0.1 dynamic-slice_compare_fusion
  243.8 0.1 fusion.20
  243.8 0.1 iota_compare_fusion
  243.9 0.1 broadcast_bitcast_fusion
  244.0 0.1 broadcast_select_fusion
  244.1 53.4 %collective-permute-done = bf16[256,3,512]{0,2,1:T(8,128)(2,1)S(1)} collective-permute-done((bf16[256,3,512]{0,2,1:T(8,128)(2,1)S(1)}, bf16[256,3,512]{0,2,1:T(8,128)(2,1)S(1)}, u32[]{:S(2)}, u32[]{:S(2)}) %collective-permute-start) | collective-permute-done | bytes 786464 | tf_op jit(solution)/shard_map/ppermute | solution.py:19
  297.5 0.5 maximum_select_fusion
  297.9 2.3 fusion.31
  300.2 2.5 fusion.13
  302.7 0.1 collective-permute-start.1
  302.8 32.1 %all-gather.5.cloned.1.call-done = bf16[512,4096]{1,0:T(8,128)(2,1)} async-done(((bf16[512,1024]{1,0:T(8,128)(2,1)}), bf16[512,4096]{1,0:T(8,128)(2,1)}) %all-gather.5.cloned.1.call-update) | async-done | bytes 4194320 | tf_op jit(solution)/shard_map/all_gather | solution.py:73
  334.9 6.6 %convolution_convert_fusion = bf16[512,4096]{1,0:T(8,128)(2,1)} fusion(bf16[512,4096]{1,0:T(8,128)(2,1)} %all-gather.5.cloned.1.call-done, bf16[512,512]{0,1:T(8,128)(2,1)S(1)} %bitcast.45, bf16[256,512]{0,1:T(8,128)(2,1)S(1)} %bitcast.48, bf16[256,512]{0,1:T(8,128)(2,1)S(1)} %collective-permute-done.1, pred[512]{0:T(512)(128)(4,1)S(1)} %broadcast_bitcast_fusion), kind=kOutput, calls=%fused_computation.1 | convolution fusion | flops 2150891520 | bytes 9437696 | tf_op jit(solution)/shard_map/dot_general | solution.py:71
  341.6 0.0 reduce-scatter.2.cloned.1.call-update
  341.6 43.3 %reduce-scatter.2.cloned.1.call-done = bf16[128,4096]{1,0:T(8,128)(2,1)} async-done(((bf16[512,4096]{1,0:T(8,128)(2,1)}), bf16[128,4096]{1,0:T(8,128)(2,1)}) %reduce-scatter.2.cloned.1.call-update) | async-done | bytes 1048592 | tf_op jit(solution)/shard_map/reduce_scatter | solution.py:76
  (9 shorter events, 0.1 us)
Async XLA Ops:
  6.5 225.8 %all-gather.3.cloned.1.call-start = ((), (), s32[]{:S(2)}) async-start(), calls=%async_computation.1 | async-start | bytes 15728640 | tf_op jit(solution)/shard_map/all_gather | solution.py:45
  11.2 323.7 %all-gather.5.cloned.1.call-start = ((), (), s32[]{:S(2)}) async-start(), calls=%async_computation.2 | async-start | bytes 5242880 | tf_op jit(solution)/shard_map/all_gather | solution.py:73
  13.6 371.3 %reduce-scatter.2.cloned.1.call-start = ((), (), s32[]{:S(2)}) async-start(), calls=%async_computation.3 | async-start | bytes 5242880 | tf_op jit(solution)/shard_map/reduce_scatter | solution.py:76
  13.6 230.0 %copy-start.1 = (s32[16]{0:T(128)S(1)}, s32[16]{0:T(128)}, u32[]{:S(2)}) copy-start(s32[16]{0:T(128)} %param.9) | copy-start | bytes 196
  13.7 230.1 %copy-start = (s32[2048]{0:T(1024)S(1)}, s32[2048]{0:T(1024)}, u32[]{:S(2)}) copy-start(s32[2048]{0:T(1024)} %param.8) | copy-start | bytes 24580
  13.7 230.1 %slice-start = ((s32[2048]{0:T(1024)}), s32[256]{0:T(256)S(1)}, s32[]{:S(2)}) async-start(s32[2048]{0:T(1024)} %param.8), calls=%async_computation.4 | async-start | bytes 2048 | tf_op jit(solution)/shard_map/slice | solution.py:52
  243.3 54.1 %collective-permute-start = (bf16[256,3,512]{0,2,1:T(8,128)(2,1)S(1)}, bf16[256,3,512]{0,2,1:T(8,128)(2,1)S(1)}, u32[]{:S(2)}, u32[]{:S(2)}) collective-permute-start(bf16[256,3,512]{0,2,1:T(8,128)(2,1)S(1)} %get-tuple-element.14), channel_id=1, source_target_pairs={{4,0},{8,4},{12,8},{0,12},{5,1},{9,5},{13,9},{1,13},{6,2},{10,6},{... | collective-permute-start | bytes 2359304 | tf_op jit(solution)/shard_map/ppermute | solution.py:19
  302.7 32.2 %collective-permute-start.1 = (bf16[256,512]{0,1:T(8,128)(2,1)S(1)}, bf16[256,512]{0,1:T(8,128)(2,1)S(1)}, u32[]{:S(2)}, u32[]{:S(2)}) collective-permute-start(bf16[256,512]{0,1:T(8,128)(2,1)S(1)} %bitcast.49), channel_id=1, source_target_pairs={{12,0},{0,4},{4,8},{8,12},{13,1},{1,5},{5,9},{9,13},{14,2},{2,6},{... | collective-permute-start | bytes 786440 | tf_op jit(solution)/shard_map/ppermute | solution.py:19
Sparse Core Ops, SparseCore 0:
  11.4 220.8 all-gather.2
  233.9 101.0 all-gather.4
  341.7 43.1 reduce-scatter.1
where the time goes:
time: 392 us; the launch traced here: 391 us
  waiting for transfers between devices  348 us (89%)
  matrix products  22.3 us (6%)
  between operations  13.2 us (3%)
  local copies, waits for them, and re-layouts  7.17 us (2%)
    all_gather x1, waiting for transfers between devices, per_device(): lax.all_gather(w_qkv, 'wide', axis=0, tiled=True)  219 us
    ppermute x2, waiting for transfers between devices, from_behind(): return lax.ppermute(block, axis, route)  53.4 us
    reduce_scatter x1, waiting for transfers between devices, per_device(): lax.psum_scatter(partial_value.astype(jnp.bfloat16), 'narrow', scatter_di...  43.3 us
    all_gather x1, waiting for transfers between devices, per_device(): lax.all_gather(own_rows, 'wide', axis=1, tiled=True)  32.1 us
    dot_general x1, matrix products, per_device(): jnp.einsum('tr,rcf->tcf', hidden, lax.all_gather(w_qkv, 'wide', axis=0, t...  10.9 us
  transfers between devices with their start and end apart: 5, of which 4 were waited for; matrix products, arithmetic and copies ran while one was open for 5% of the time, Pallas kernels for 0%

commit v1 on v0

v1 whole, which is shorter than its diff:
```python
import functools
import math

import jax
import jax.numpy as jnp
from jax import lax
from jax.experimental import pallas as pl
from jax.experimental.pallas import tpu as pltpu
from jax.sharding import PartitionSpec as P

HEAD_DIM = 128
GROUP = 512
SHIFT = 256

masked_out = -1e30
MESH = pl.DeviceIdType.MESH


def gather_kernel(
    n, chunks, hidden_ref, wq_ref, wo_ref, proj_ref, wo_out,
    wbuf, acc, local_sem,
    send_r, send_l, send_yr, send_yl, recv_r, recv_l, recv_yr, recv_yl,
):
    me = lax.axis_index("wide")
    y = lax.axis_index("groups")
    other = 1 - y
    depth = wq_ref.shape[1]
    rows = depth // chunks
    steps = (n - 1) * chunks

    barrier = pltpu.get_barrier_semaphore()

    @pl.when(me > 0)
    def _():
        pl.semaphore_signal(barrier, inc=1, device_id={"wide": me - 1}, device_id_type=MESH)

    @pl.when(me < n - 1)
    def _():
        pl.semaphore_signal(barrier, inc=1, device_id={"wide": me + 1}, device_id_type=MESH)

    pl.semaphore_signal(barrier, inc=1, device_id={"groups": other}, device_id_type=MESH)
    has_left = jnp.where(me > 0, 1, 0)
    has_right = jnp.where(me < n - 1, 1, 0)
    own = [
        pltpu.make_async_copy(
            wq_ref.at[h], wbuf.at[h, pl.ds(pl.multiple_of(me * depth, depth), depth)], local_sem.at[h]
        )
        for h in range(2)
    ]
    own.append(pltpu.make_async_copy(wo_ref, wo_out.at[me], local_sem.at[2]))
    for copy in own:
        copy.start()
    pl.semaphore_wait(barrier, has_left + has_right + 1)

    def w_at(shard, half, c):
        start = pl.multiple_of(shard * depth + c * rows, rows)
        return wbuf.at[half, pl.ds(start, rows)]

    def wq_own(c):
        return wq_ref.at[y, pl.ds(pl.multiple_of(c * rows, rows), rows)]

    def o_at(shard, half):
        return wo_out.at[shard, half]

    def remote(src, dst, send, recv, slot, device):
        return pltpu.make_async_remote_copy(
            src_ref=src, dst_ref=dst, send_sem=send.at[slot], recv_sem=recv.at[slot],
            device_id=device, device_id_type=MESH,
        )

    right, left, across = {"wide": me + 1}, {"wide": me - 1}, {"groups": other}

    def pick(t):
        return t // chunks, lax.rem(t, chunks)

    def send_right(t, src, shard):
        s, c = pick(t)
        return remote(src, w_at(shard, y, c), send_r, recv_r, t, right)

    def send_left(t, src, shard):
        s, c = pick(t)
        return remote(src, w_at(shard, y, c), send_l, recv_l, t, left)

    @pl.loop(0, chunks)
    def _(c):
        @pl.when(me < n - 1)
        def _():
            send_right(c, wq_own(c), me).start()

        @pl.when(me > 0)
        def _():
            send_left(c, wq_own(c), me).start()

    acc[...] = jnp.zeros_like(acc)
    own[0].wait()
    own[1].wait()

    def add(shard, half, c):
        start = pl.multiple_of(shard * depth + c * rows, rows)
        acc[half] += jnp.dot(
            hidden_ref[:, pl.ds(start, rows)], wbuf[half, pl.ds(start, rows)],
            preferred_element_type=jnp.float32,
        )

    @pl.loop(0, 2 * chunks)
    def _(i):
        add(me, i // chunks, lax.rem(i, chunks))

    def from_across(t):
        s, c = pick(t)

        @pl.when(me - 1 - s >= 0)
        def _():
            ref = w_at(me - 1 - s, other, c)
            remote(ref, ref, send_yr, recv_yr, t, across).wait_recv()
            add(me - 1 - s, other, c)

        @pl.when(me + 1 + s <= n - 1)
        def _():
            ref = w_at(me + 1 + s, other, c)
            remote(ref, ref, send_yl, recv_yl, t, across).wait_recv()
            add(me + 1 + s, other, c)

    @pl.loop(0, steps)
    def _(t):
        s, c = pick(t)

        @pl.when(me - 1 - s >= 0)
        def _():
            ref = w_at(me - 1 - s, y, c)
            remote(ref, ref, send_r, recv_r, t, left).wait_recv()

            @pl.when(me < n - 1)
            def _():
                send_right(t + chunks, ref, me - 1 - s).start()

            remote(ref, ref, send_yr, recv_yr, t, across).start()

        @pl.when(me + 1 + s <= n - 1)
        def _():
            ref = w_at(me + 1 + s, y, c)
            remote(ref, ref, send_l, recv_l, t, right).wait_recv()

            @pl.when(me > 0)
            def _():
                send_left(t + chunks, ref, me + 1 + s).start()

            remote(ref, ref, send_yl, recv_yl, t, across).start()

        @pl.when(me - 1 - s >= 0)
        def _():
            add(me - 1 - s, y, c)

        @pl.when(me + 1 + s <= n - 1)
        def _():
            add(me + 1 + s, y, c)

        @pl.when(t > 0)
        def _():
            from_across(t - 1)

    @pl.when(me < n - 1)
    def _():
        remote(wo_ref.at[y], o_at(me, y), send_r, recv_r, steps, right).start()

    @pl.when(me > 0)
    def _():
        remote(wo_ref.at[y], o_at(me, y), send_l, recv_l, steps, left).start()

    from_across(steps - 1)
    proj_ref[...] = acc[...].astype(jnp.bfloat16)

    @pl.loop(0, n - 1)
    def _(s):
        t = steps + s

        @pl.when(me - 1 - s >= 0)
        def _():
            ref = o_at(me - 1 - s, y)
            remote(ref, ref, send_r, recv_r, t, left).wait_recv()

            @pl.when(me < n - 1)
            def _():
                remote(ref, ref, send_r, recv_r, t + 1, right).start()

            remote(ref, ref, send_yr, recv_yr, t, across).start()

        @pl.when(me + 1 + s <= n - 1)
        def _():
            ref = o_at(me + 1 + s, y)
            remote(ref, ref, send_l, recv_l, t, right).wait_recv()

            @pl.when(me > 0)
            def _():
                remote(ref, ref, send_l, recv_l, t + 1, left).start()

            remote(ref, ref, send_yl, recv_yl, t, across).start()

    own[2].wait()

    @pl.loop(0, n - 1)
    def _(s):
        t = steps + s

        @pl.when(me - 1 - s >= 0)
        def _():
            ref = o_at(me - 1 - s, other)
            remote(ref, ref, send_yr, recv_yr, t, across).wait_recv()
            ref = o_at(me - 1 - s, y)
            remote(ref, ref, send_yr, recv_yr, t, across).wait_send()

        @pl.when(me + 1 + s <= n - 1)
        def _():
            ref = o_at(me + 1 + s, other)
            remote(ref, ref, send_yl, recv_yl, t, across).wait_recv()
            ref = o_at(me + 1 + s, y)
            remote(ref, ref, send_yl, recv_yl, t, across).wait_send()

        @pl.when(jnp.logical_and(me - s >= 0, me < n - 1))
        def _():
            ref = o_at(me - s, y)
            remote(ref, ref, send_r, recv_r, t, right).wait_send()

        @pl.when(jnp.logical_and(me + s <= n - 1, me > 0))
        def _():
            ref = o_at(me + s, y)
            remote(ref, ref, send_l, recv_l, t, left).wait_send()

    @pl.loop(0, steps)
    def _(t):
        s, c = pick(t)

        @pl.when(me - 1 - s >= 0)
        def _():
            ref = w_at(me - 1 - s, y, c)
            remote(ref, ref, send_yr, recv_yr, t, across).wait_send()

        @pl.when(me + 1 + s <= n - 1)
        def _():
            ref = w_at(me + 1 + s, y, c)
            remote(ref, ref, send_yl, recv_yl, t, across).wait_send()

        @pl.when(jnp.logical_and(me - s >= 0, me < n - 1))
        def _():
            ref = w_at(me - s, y, c)
            remote(ref, ref, send_r, recv_r, t, right).wait_send()

        @pl.when(jnp.logical_and(me + s <= n - 1, me > 0))
        def _():
            ref = w_at(me + s, y, c)
            remote(ref, ref, send_l, recv_l, t, left).wait_send()


def gather_project(hidden, wq, wo):
    n = lax.axis_size("wide")
    tok, width = hidden.shape
    half = wq.shape[2]
    chunks = max(1, wq.shape[1] // 256)
    slots = (n - 1) * (chunks + 1)
    vmem = pl.BlockSpec(memory_space=pltpu.VMEM)
    hbm = pl.BlockSpec(memory_space=pl.ANY)
    return pl.pallas_call(
        functools.partial(gather_kernel, n, chunks),
        out_shape=(
            jax.ShapeDtypeStruct((2, tok, half), jnp.bfloat16),
            jax.ShapeDtypeStruct((n,) + wo.shape, jnp.bfloat16),
        ),
        in_specs=[vmem, hbm, hbm],
        out_specs=(vmem, vmem),
        scratch_shapes=[
            pltpu.VMEM((2, width, half), jnp.bfloat16),
            pltpu.VMEM((2, tok, half), jnp.float32),
            pltpu.SemaphoreType.DMA((3,)),
        ]
        + [pltpu.SemaphoreType.DMA((slots,)) for _ in range(8)],
        compiler_params=pltpu.CompilerParams(
            collective_id=0, has_side_effects=True, vmem_limit_bytes=56 * 1024 * 1024
        ),
    )(hidden, wq, wo)


def attend_kernel(heads, blocks, q_ref, k_ref, v_ref, segq_ref, segk_ref, out_ref):
    rows = lax.broadcasted_iota(jnp.int32, (SHIFT, 2 * SHIFT), 0)
    cols = lax.broadcasted_iota(jnp.int32, (SHIFT, 2 * SHIFT), 1)
    causal = cols <= rows + SHIFT
    for h in range(heads):
        lanes = slice(h * HEAD_DIM, (h + 1) * HEAD_DIM)
        for b in range(blocks):
            mine = slice(b * SHIFT, (b + 1) * SHIFT)
            seen = slice(b * SHIFT, (b + 2) * SHIFT)
            scores = lax.dot_general(
                q_ref[mine, lanes], k_ref[seen, lanes], (((1,), (1,)), ((), ())),
                preferred_element_type=jnp.float32,
            ) * (1.0 / math.sqrt(HEAD_DIM))
            allowed = causal & (segq_ref[mine, :] == segk_ref[h, b])
            scores = jnp.where(allowed, scores, masked_out)
            exponent = jnp.exp(scores - jnp.max(scores, axis=-1, keepdims=True))
            weights = exponent / jnp.sum(exponent, axis=-1, keepdims=True)
            out_ref[mine, lanes] = jnp.dot(
                weights.astype(jnp.bfloat16), v_ref[seen, lanes], preferred_element_type=jnp.float32
            ).astype(jnp.bfloat16)


def per_device(hidden, w_qkv, w_out, seg_ids, shift_heads):
    n = lax.axis_size("wide")
    tok_rows = hidden.shape[0]
    depth, _, local_f = w_qkv.shape
    heads_here = local_f // HEAD_DIM
    blocks = tok_rows // SHIFT
    narrow_idx = lax.axis_index("narrow")
    first_tok = lax.axis_index("wide") * tok_rows
    shifted = lax.dynamic_slice_in_dim(shift_heads, narrow_idx * heads_here, heads_here) > 0

    half = 3 * local_f // 2
    wq = w_qkv.reshape(depth, 2, half).transpose(1, 0, 2)
    own_rows = lax.dynamic_slice_in_dim(w_out, narrow_idx * local_f, local_f, 0)
    wo = own_rows.reshape(2, local_f // 2, -1)
    proj, wo_all = gather_project(hidden, wq, wo)
    projected = jnp.concatenate([proj[0], proj[1]], 1)
    q = projected[:, :local_f]
    kv = projected[:, local_f:]
    before = lax.ppermute(kv[tok_rows - SHIFT :], "wide", [(i, (i + 1) % n) for i in range(n)])
    kv = jnp.concatenate([before, kv], 0)

    doubled = jnp.concatenate([seg_ids[-SHIFT:], seg_ids], 0)
    seg_here = lax.dynamic_slice_in_dim(doubled, first_tok, tok_rows + SHIFT)
    seg_q = seg_here[SHIFT:, None]
    windows = jnp.stack([seg_here[b * SHIFT : (b + 2) * SHIFT] for b in range(blocks)])
    odd = (jnp.arange(blocks) % 2 == 1)[None, :, None]
    reaches = (shifted[:, None, None] != odd) | (jnp.arange(2 * SHIFT) >= SHIFT)[None, None, :]
    seg_k = jnp.where(reaches, windows[None], -1)[:, :, None, :]

    vmem = pl.BlockSpec(memory_space=pltpu.VMEM)
    attended = pl.pallas_call(
        functools.partial(attend_kernel, heads_here, blocks),
        out_shape=jax.ShapeDtypeStruct((tok_rows, local_f), jnp.bfloat16),
        in_specs=[vmem] * 5,
        out_specs=vmem,
    )(q, kv[:, :local_f], kv[:, local_f:], seg_q, seg_k)

    partial_value = jnp.einsum(
        "tf,nfc->tnc", attended, wo_all.reshape(n, local_f, -1), preferred_element_type=jnp.float32
    ).astype(jnp.bfloat16).reshape(tok_rows, -1)
    return lax.psum_scatter(partial_value, "narrow", scatter_dimension=0, tiled=True)


def solution(mesh):
    placed = (
        P(("groups", "wide"), None),
        P("wide", None, "narrow"),
        P(None, "wide"),
        P("groups"),
        P(),
    )
    return jax.shard_map(
        per_device,
        mesh=mesh,
        in_specs=placed,
        out_specs=P(("groups", "wide", "narrow"), None),
        check_vma=False,
    )
```

time: 392 us -> 273 us (0.70)
  waiting for transfers between devices: 348 us -> 54 us
  Pallas kernels: 0 us -> 172 us
  local copies, waits for them, and re-layouts: 7.17 us -> 25.4 us
  matrix products: 22.3 us -> 6.69 us
    all_gather x2 -> x0, waiting for transfers between devices: 251 us -> none  [the longest x1 219 us: per_device(): lax.all_gather(w_qkv, 'wide', axis=0, tiled=True)]
    pallas_call x0 -> x2, Pallas kernels: none -> 172 us  [the longest x1 166 us: gather_project(): pl.pallas_call(functools.partial(gather_kernel, n, chunks), out_shape=(ja...]
    ppermute x2 -> x1, waiting for transfers between devices: 53.4 us -> 10.3 us  [per_device(): lax.ppermute(kv[tok_rows - SHIFT:], 'wide', [(i, (i + 1) % n) for i in ra...]
    dot_general x3 -> x1, matrix products: 20 us -> 6.69 us  [per_device(): jnp.einsum('tf,nfc->tnc', attended, wo_all.reshape(n, local_f, -1), prefe...]
    convert_element_type x0 -> x1, local copies, waits for them, and re-layouts: none -> 6.2 us  [per_device(): partial_value = jnp.einsum('tf,nfc->tnc', attended, wo_all.reshape(n, loc...]
    unnamed x5 -> x6, local copies, waits for them, and re-layouts: 4.69 us -> 9.67 us
  transfers between devices with their start and end apart: 5 -> 2, of which waited for: 4 -> 2; matrix products, arithmetic and copies ran while one was open for 5% -> 1% of each run, Pallas kernels for 0% -> 0%
where the time goes in v1:
time: 273 us
  Pallas kernels  172 us (63%)
  waiting for transfers between devices  54 us (20%)
  local copies, waits for them, and re-layouts  25.4 us (9%)
  between operations  13.5 us (5%)
  matrix products  6.69 us (2%)
    pallas_call x1, Pallas kernels, gather_project(): pl.pallas_call(functools.partial(gather_kernel, n, chunks), out_shape=(ja...  166 us
    reduce_scatter x1, waiting for transfers between devices, per_device(): lax.psum_scatter(partial_value, 'narrow', scatter_dimension=0, tiled=True)  43.7 us
    ppermute x1, waiting for transfers between devices, per_device(): lax.ppermute(kv[tok_rows - SHIFT:], 'wide', [(i, (i + 1) % n) for i in ra...  10.3 us
    unnamed x6, local copies, waits for them, and re-layouts  9.67 us
    dot_general x1, matrix products, per_device(): jnp.einsum('tf,nfc->tnc', attended, wo_all.reshape(n, local_f, -1), prefe...  6.69 us
    convert_element_type x1, local copies, waits for them, and re-layouts, per_device(): partial_value = jnp.einsum('tf,nfc->tnc', attended, wo_all.reshape(n, loc...  6.2 us
    pallas_call x1, Pallas kernels, per_device(): pl.pallas_call(functools.partial(attend_kernel, heads_here, blocks), out_...  6.2 us
  transfers between devices with their start and end apart: 2, of which 2 were waited for; matrix products, arithmetic and copies ran while one was open for 1% of the time, Pallas kernels for 0%

profile of v1, /device:TPU:0, one launch (start us, length us, event | category | flops | bytes accessed | tf_op | source)
XLA Modules:
  0.0 272.7 jit_solution(9980765543054882388)
XLA Ops:
  6.5 3.2 %copy.11 = bf16[1024,3,512]{0,2,1:T(8,128)(2,1)S(1)} copy(bf16[1024,3,512]{2,0,1:T(8,128)(2,1)} %param.6) | data formatting | bytes 6291456 | tf_op args[1]
  9.7 2.8 %copy.12 = bf16[1024,2,768]{2,0,1:T(8,128)(2,1)} copy(bf16[1024,2,768]{0,2,1:T(8,128)(2,1)S(1)} %bitcast.18) | data formatting | bytes 6291456 | tf_op jit(solution)/shard_map/reshape | solution.py:315
  12.5 2.3 constant_dynamic-slice_fusion
  14.8 165.7 %shard_map.55 = (bf16[2,512,768]{2,1,0:T(8,128)(2,1)}, bf16[4,2,256,1024]{3,2,1,0:T(8,128)(2,1)}) custom-call(bf16[512,4096]{1,0:T(8,128)(2,1)} %hidden_ref.1, bf16[2,1024,768]{2,1,0:T(8,128)(2,1)} %bitcast.19, bf16[2,256,1024]{2,1,0:T(8,128)(2,1)} %bitcast.20), custom_call_target="tpu_custom_call" | custom-call | tf_op jit(solution)/shard_map/pallas_call | solution.py:262
  180.5 0.0 copy-start
  180.5 0.0 copy-start.1
  180.5 1.5 slice_bitcast_fusion
  182.0 0.1 pad_maximum_fusion.1
  182.1 0.1 collective-permute-start
  182.2 0.8 slice.42.q_ref
  183.0 0.1 fusion.2
  183.1 0.9 copy.13.segq_ref
  184.0 0.1 dynamic-slice_compare_fusion
  184.1 0.1 broadcast_compare_fusion
  184.1 0.7 or_select_fusion.segk_ref
  184.8 10.3 %collective-permute-done = bf16[256,1024]{1,0:T(8,128)(2,1)S(1)} collective-permute-done((bf16[256,1024]{1,0:T(8,128)(2,1)S(1)}, bf16[256,1024]{1,0:T(8,128)(2,1)S(1)}, u32[]{:S(2)}, u32[]{:S(2)}) %collective-permute-start) | collective-permute-done | bytes 524320 | tf_op jit(solution)/shard_map/ppermute | solution.py:322
  195.1 0.2 fusion
  195.3 1.3 fusion.4
  196.6 6.2 %shard_map.56 = bf16[512,512]{1,0:T(8,128)(2,1)} custom-call(bf16[512,512]{1,0:T(8,128)(2,1)} %slice.42.q_ref, bf16[768,512]{1,0:T(8,128)(2,1)} %get-tuple-element.10.k_ref, bf16[768,512]{1,0:T(8,128)(2,1)} %get-tuple-element.9.v_ref, s32[512,1]{1,0:T(8,128)} %copy.13.segq_ref, s32[4,2,1,512]{3,2,1,0:T(1,128)} %or_select_fusion.segk_ref), custom_call_target="tpu_custom_call" | custom-call | tf_op jit(solution)/shard_map/pallas_call | solution.py:334
  202.8 6.7 %convolution_convert_fusion = bf16[512,4,1024]{2,0,1:T(8,128)(2,1)} fusion(bf16[4,512,1024]{2,1,0:T(8,128)(2,1)} %bitcast.24, bf16[512,512]{1,0:T(8,128)(2,1)} %shard_map.56), kind=kOutput, calls=%fused_computation | convolution fusion | flops 2149580800 | bytes 8912896 | tf_op jit(solution)/shard_map/tf,nfc->tnc/dot_general | solution.py:341
  209.4 6.2 %copy.14 = bf16[512,4,1024]{0,2,1:T(8,128)(2,1)} copy(bf16[512,4,1024]{2,0,1:T(8,128)(2,1)} %convolution_convert_fusion) | data formatting | bytes 8388608 | tf_op jit(solution)/shard_map/convert_element_type | solution.py:343
  215.7 6.5 %copy.16 = bf16[512,4096]{1,0:T(8,128)(2,1)} copy(bf16[512,4096]{0,1:T(8,128)(2,1)} %bitcast.17) | data formatting | bytes 8388608
  222.1 0.0 reduce-scatter.4.cloned.1.call-update
  222.2 43.7 %reduce-scatter.4.cloned.1.call-done = bf16[128,4096]{1,0:T(8,128)(2,1)} async-done(((bf16[512,4096]{1,0:T(8,128)(2,1)}), bf16[128,4096]{1,0:T(8,128)(2,1)}) %reduce-scatter.4.cloned.1.call-update) | async-done | bytes 1048592 | tf_op jit(solution)/shard_map/reduce_scatter | solution.py:344
  (8 shorter events, 0.0 us)
Async XLA Ops:
  6.5 259.3 %reduce-scatter.4.cloned.1.call-start = ((), (), s32[]{:S(2)}) async-start(), calls=%async_computation.1 | async-start | bytes 5242880 | tf_op jit(solution)/shard_map/reduce_scatter | solution.py:344
  180.5 2.5 copy-start
  180.5 3.4 %copy-start.1 = (s32[16]{0:T(128)S(1)}, s32[16]{0:T(128)}, u32[]{:S(2)}) copy-start(s32[16]{0:T(128)} %param.9) | copy-start | bytes 196
  182.1 13.0 %collective-permute-start = (bf16[256,1024]{1,0:T(8,128)(2,1)S(1)}, bf16[256,1024]{1,0:T(8,128)(2,1)S(1)}, u32[]{:S(2)}, u32[]{:S(2)}) collective-permute-start(bf16[256,1024]{1,0:T(8,128)(2,1)S(1)} %pad_maximum_fusion.1), channel_id=1, source_target_pairs={{0,4},{4,8},{8,12},{12,0},{1,5},{5,9},{9,13},{13,1},{2,6},{6,10},{... | collective-permute-start | bytes 1572872 | tf_op jit(solution)/shard_map/ppermute | solution.py:322
Sparse Core Ops, SparseCore 0:
  222.3 43.5 reduce-scatter.3

commit v2 on v0

v2 whole, which is shorter than its diff:
```python
import functools
import math

import jax
import jax.numpy as jnp
from jax import lax
from jax.experimental import pallas as pl
from jax.experimental.pallas import tpu as pltpu
from jax.sharding import PartitionSpec as P

HEAD_DIM = 128
GROUP = 512
SHIFT = 256

masked_out = -1e30
MESH = pl.DeviceIdType.MESH
ROWS = 128
WO_CHUNKS = 2


def layer_kernel(
    n, narrow, chunks, wo_chunks,
    hidden_ref, wq_ref, wo_ref, segq_ref, segk_ref, out_ref,
    wbuf, acc, wo_buf, q_buf, kv_buf, att, part, pair_in, pair_sum, far_in,
    own_sem,
    qs_r, qs_l, qr, qs_y, qr_y,
    os_r, os_l, o_r, os_y, or_y,
    kv_sem, pair_s, pair_r, far_s, far_r,
):
    me = lax.axis_index("wide")
    y = lax.axis_index("groups")
    spot = lax.axis_index("narrow")
    other = 1 - y
    across_n = narrow // 2
    high, low = spot // 2, lax.rem(spot, 2)
    depth = wq_ref.shape[1]
    half = wbuf.shape[3]
    tok = hidden_ref.shape[0]
    rows = depth // chunks
    steps = (n - 1) * chunks
    wo_rows = wo_buf.shape[2] // wo_chunks
    cols = wo_buf.shape[3]
    blocks = tok // SHIFT
    per_half = half // HEAD_DIM
    has_left, has_right = me > 0, me < n - 1
    right, left = {"wide": me + 1}, {"wide": me - 1}
    after, before = {"wide": lax.rem(me + 1, n)}, {"wide": lax.rem(me + n - 1, n)}
    opposite = {"groups": other}
    pair = {"narrow": high * 2 + 1 - low}
    far = [{"narrow": lax.rem(high + d, across_n) * 2 + low} for d in range(1, across_n)]
    far_from = [{"narrow": lax.rem(high + across_n - d, across_n) * 2 + low} for d in range(1, across_n)]

    barrier = pltpu.get_barrier_semaphore()
    greeted = [after, before, opposite, pair] + far
    for device in greeted:
        pl.semaphore_signal(barrier, inc=1, device_id=device, device_id_type=MESH)

    def w_at(shard, part_of, c):
        start = pl.multiple_of(shard * depth + c * rows, rows)
        return wbuf.at[part_of, :, pl.ds(start, rows)]

    def wq_own(c):
        return wq_ref.at[
            :, pl.ds(pl.multiple_of(c * rows, rows), rows), pl.ds(pl.multiple_of(y * half, half), half)
        ]

    def o_at(shard, part_of, c):
        return wo_buf.at[shard, part_of, pl.ds(pl.multiple_of(c * wo_rows, wo_rows), wo_rows)]

    def wo_own(c):
        return wo_ref.at[spot, y, pl.ds(pl.multiple_of(c * wo_rows, wo_rows), wo_rows)]

    def remote(src, dst, send, recv, device):
        return pltpu.make_async_remote_copy(
            src_ref=src, dst_ref=dst, send_sem=send, recv_sem=recv,
            device_id=device, device_id_type=MESH,
        )

    def q_right(shard, c, src=None):
        dst = w_at(shard, y, c)
        return remote(dst if src is None else src, dst, qs_r.at[shard, c], qr.at[shard, c], right)

    def q_left(shard, c, src=None):
        dst = w_at(shard, y, c)
        return remote(dst if src is None else src, dst, qs_l.at[shard, c], qr.at[shard, c], left)

    def q_across(shard, c, part_of):
        ref = w_at(shard, part_of, c)
        return remote(ref, ref, qs_y.at[shard, c], qr_y.at[shard, c], opposite)

    def o_right(shard, c, src=None):
        dst = o_at(shard, y, c)
        return remote(dst if src is None else src, dst, os_r.at[shard, c], o_r.at[shard, c], right)

    def o_left(shard, c, src=None):
        dst = o_at(shard, y, c)
        return remote(dst if src is None else src, dst, os_l.at[shard, c], o_r.at[shard, c], left)

    def o_across(shard, c, part_of):
        ref = o_at(shard, part_of, c)
        return remote(ref, ref, os_y.at[shard, c], or_y.at[shard, c], opposite)

    own = [
        pltpu.make_async_copy(
            wq_ref.at[:, :, pl.ds(h * half, half)],
            wbuf.at[h, :, pl.ds(pl.multiple_of(me * depth, depth), depth)],
            own_sem.at[h],
        )
        for h in range(2)
    ]
    own.append(pltpu.make_async_copy(wo_ref.at[spot], wo_buf.at[me], own_sem.at[2]))
    for copy in own:
        copy.start()
    pl.semaphore_wait(barrier, len(greeted))

    @pl.loop(0, chunks)
    def _(c):
        @pl.when(has_right)
        def _():
            q_right(me, c, wq_own(c)).start()

        @pl.when(has_left)
        def _():
            q_left(me, c, wq_own(c)).start()

    acc[...] = jnp.zeros_like(acc)
    own[0].wait()
    own[1].wait()

    def add(shard, part_of, c):
        start = pl.multiple_of(shard * depth + c * rows, rows)
        piece = hidden_ref[:, pl.ds(start, rows)]
        for i in range(3):
            acc[part_of, i] += jnp.dot(
                piece, wbuf[part_of, i, pl.ds(start, rows)], preferred_element_type=jnp.float32
            )

    @pl.loop(0, 2 * chunks)
    def _(i):
        add(me, i // chunks, lax.rem(i, chunks))

    def add_across(t):
        s, c = t // chunks, lax.rem(t, chunks)
        for there, shard in ((me - 1 - s >= 0, me - 1 - s), (me + 1 + s <= n - 1, me + 1 + s)):
            @pl.when(there)
            def _():
                q_across(shard, c, other).wait_recv()
                add(shard, other, c)

    @pl.loop(0, steps)
    def _(t):
        s, c = t // chunks, lax.rem(t, chunks)

        @pl.when(me - 1 - s >= 0)
        def _():
            q_right(me - 1 - s, c).wait_recv()

            @pl.when(has_right)
            def _():
                q_right(me - 1 - s, c).start()

            q_across(me - 1 - s, c, y).start()

        @pl.when(me + 1 + s <= n - 1)
        def _():
            q_left(me + 1 + s, c).wait_recv()

            @pl.when(has_left)
            def _():
                q_left(me + 1 + s, c).start()

            q_across(me + 1 + s, c, y).start()

        for there, shard in ((me - 1 - s >= 0, me - 1 - s), (me + 1 + s <= n - 1, me + 1 + s)):
            @pl.when(there)
            def _():
                add(shard, y, c)

        @pl.when(t > 0)
        def _():
            add_across(t - 1)

    add_across(steps - 1)
    for h in range(2):
        q_buf[h] = acc[h, 0].astype(jnp.bfloat16)
        for i in range(2):
            kv_buf[h, i, SHIFT:] = acc[h, 1 + i].astype(jnp.bfloat16)

    kv_copy = remote(
        kv_buf.at[:, :, pl.ds(tok, SHIFT)], kv_buf.at[:, :, pl.ds(0, SHIFT)],
        kv_sem.at[0], kv_sem.at[1], after,
    )
    kv_copy.start()

    @pl.loop(0, wo_chunks)
    def _(c):
        @pl.when(has_right)
        def _():
            o_right(me, c, wo_own(c)).start()

        @pl.when(has_left)
        def _():
            o_left(me, c, wo_own(c)).start()

    causal = lax.broadcasted_iota(jnp.int32, (SHIFT, 2 * SHIFT), 1) <= (
        lax.broadcasted_iota(jnp.int32, (SHIFT, 2 * SHIFT), 0) + SHIFT
    )

    def attend(h, b):
        lanes = slice((h % per_half) * HEAD_DIM, (h % per_half + 1) * HEAD_DIM)
        mine, seen = slice(b * SHIFT, (b + 1) * SHIFT), slice(b * SHIFT, (b + 2) * SHIFT)
        keys, values = kv_buf.at[h // per_half, 0], kv_buf.at[h // per_half, 1]
        scores = lax.dot_general(
            q_buf[h // per_half, mine, lanes], keys[seen, lanes], (((1,), (1,)), ((), ())),
            preferred_element_type=jnp.float32,
        ) * (1.0 / math.sqrt(HEAD_DIM))
        allowed = causal & (segq_ref[mine, :] == segk_ref[h, b])
        scores = jnp.where(allowed, scores, masked_out)
        exponent = jnp.exp(scores - jnp.max(scores, axis=-1, keepdims=True))
        weights = exponent / jnp.sum(exponent, axis=-1, keepdims=True)
        att[mine, h * HEAD_DIM : (h + 1) * HEAD_DIM] = jnp.dot(
            weights.astype(jnp.bfloat16), values[seen, lanes], preferred_element_type=jnp.float32
        ).astype(jnp.bfloat16)

    least = jnp.minimum(me, n - 1 - me)

    def block_of(k):
        turn = (k + 1) // 2
        near = jnp.where(lax.rem(k, 2) == 1, me - turn, me + turn)
        rest = jnp.where(me > least, me - (k - least), me + (k - least))
        return jnp.where(k <= 2 * least, near, rest)

    def pass_on(k):
        shard = block_of(k)

        @pl.loop(0, wo_chunks)
        def _(c):
            o_right(shard, c).wait_recv()

            @pl.when(jnp.logical_and(shard < me, has_right))
            def _():
                o_right(shard, c).start()

            @pl.when(jnp.logical_and(shard > me, has_left))
            def _():
                o_left(shard, c).start()

            o_across(shard, c, y).start()

    def pair_copy(shard, a):
        return remote(
            part.at[shard, a * 2 + 1 - low], pair_in.at[shard, a],
            pair_s.at[shard, a], pair_r.at[shard, a], pair,
        )

    def far_copy(shard, d):
        a = lax.rem(high + d, across_n)
        return remote(
            pair_sum.at[shard, a], far_in.at[shard, d - 1],
            far_s.at[shard, d - 1], far_r.at[shard, d - 1], far[d - 1],
        )

    def far_arrival(shard, d):
        return remote(
            pair_sum.at[shard, high], far_in.at[shard, d - 1],
            far_s.at[shard, d - 1], far_r.at[shard, d - 1], far_from[d - 1],
        )

    def multiply(k):
        shard = block_of(k)
        width = att.shape[1] // 2
        share = tok // narrow
        for p in range(narrow):
            a_rows = att[p * share : (p + 1) * share, :]
            total = jnp.dot(a_rows[:, :width], wo_buf[shard, 0], preferred_element_type=jnp.float32)
            total += jnp.dot(a_rows[:, width:], wo_buf[shard, 1], preferred_element_type=jnp.float32)
            part[shard, p] = total.astype(jnp.bfloat16)
        for a in range(across_n):
            pair_copy(shard, a).start()

    def sum_pair(k):
        shard = block_of(k)
        for a in range(across_n):
            pair_copy(shard, a).wait_recv()
            total = part[shard, a * 2 + low].astype(jnp.float32) + pair_in[shard, a].astype(jnp.float32)
            pair_sum[shard, a] = total.astype(jnp.bfloat16)
        for d in range(1, across_n):
            far_copy(shard, d).start()

    def finish(k):
        shard = block_of(k)
        total = part[shard, high * 2 + low].astype(jnp.float32) + pair_in[shard, high].astype(jnp.float32)
        for d in range(1, across_n):
            far_arrival(shard, d).wait_recv()
            total += far_in[shard, d - 1].astype(jnp.float32)
        out_ref[:, pl.ds(pl.multiple_of(shard * cols, cols), cols)] = total.astype(out_ref.dtype)

    heads = 2 * per_half
    for b in range(1, blocks):
        for h in range(heads):
            attend(h, b)
    pass_on(1)
    kv_copy.wait_recv()
    for h in range(heads):
        attend(h, 0)
    own[2].wait()
    multiply(0)

    @pl.loop(1, n)
    def _(k):
        @pl.when(k > 1)
        def _():
            pass_on(k)

        sum_pair(k - 1)

        @pl.when(k > 1)
        def _():
            finish(k - 2)

        shard = block_of(k)

        @pl.loop(0, wo_chunks)
        def _(c):
            o_across(shard, c, other).wait_recv()

        multiply(k)

    sum_pair(n - 1)
    finish(n - 2)
    finish(n - 1)

    kv_copy.wait_send()

    @pl.loop(0, n)
    def _(shard):
        for a in range(across_n):
            pair_copy(shard, a).wait_send()
        for d in range(1, across_n):
            far_copy(shard, d).wait_send()
        goes_right = jnp.logical_and(shard <= me, has_right)
        goes_left = jnp.logical_and(shard >= me, has_left)
        for count, to_right, to_left, to_other in (
            (chunks, q_right, q_left, q_across), (wo_chunks, o_right, o_left, o_across)
        ):
            @pl.loop(0, count)
            def _(c):
                @pl.when(goes_right)
                def _():
                    to_right(shard, c).wait_send()

                @pl.when(goes_left)
                def _():
                    to_left(shard, c).wait_send()

                @pl.when(shard != me)
                def _():
                    to_other(shard, c, y).wait_send()


def layer(hidden, wq, wo, seg_q, seg_k):
    n, narrow = lax.axis_size("wide"), lax.axis_size("narrow")
    tok, width = hidden.shape
    half = wq.shape[2] // 2
    chunks = max(1, wq.shape[1] // ROWS)
    wo_chunks = WO_CHUNKS
    cols = wo.shape[3]
    share = tok // narrow
    vmem = pl.BlockSpec(memory_space=pltpu.VMEM)
    hbm = pl.BlockSpec(memory_space=pl.ANY)
    dma = pltpu.SemaphoreType.DMA
    bf16 = jnp.bfloat16
    return pl.pallas_call(
        functools.partial(layer_kernel, n, narrow, chunks, wo_chunks),
        out_shape=jax.ShapeDtypeStruct((share, n * cols), bf16),
        in_specs=[vmem, hbm, hbm, vmem, vmem],
        out_specs=vmem,
        scratch_shapes=[
            pltpu.VMEM((2, 3, width, half), bf16),
            pltpu.VMEM((2, 3, tok, half), jnp.float32),
            pltpu.VMEM((n,) + wo.shape[1:], bf16),
            pltpu.VMEM((2, tok, half), bf16),
            pltpu.VMEM((2, 2, tok + SHIFT, half), bf16),
            pltpu.VMEM((tok, 2 * half), bf16),
            pltpu.VMEM((n, narrow, share, cols), bf16),
            pltpu.VMEM((n, narrow // 2, share, cols), bf16),
            pltpu.VMEM((n, narrow // 2, share, cols), bf16),
            pltpu.VMEM((n, max(1, narrow // 2 - 1), share, cols), bf16),
            dma((3,)),
        ]
        + [dma((n, chunks))] * 5
        + [dma((n, wo_chunks))] * 5
        + [dma((2,))]
        + [dma((n, narrow // 2))] * 2
        + [dma((n, max(1, narrow // 2 - 1)))] * 2,
        compiler_params=pltpu.CompilerParams(
            collective_id=0, has_side_effects=True, vmem_limit_bytes=58 * 1024 * 1024
        ),
    )(hidden, wq, wo, seg_q, seg_k)


def per_device(hidden, w_qkv, w_out, seg_ids, shift_heads):
    tok_rows = hidden.shape[0]
    local_f = w_qkv.shape[2]
    heads_here = local_f // HEAD_DIM
    blocks = tok_rows // SHIFT
    narrow = lax.axis_size("narrow")
    first_tok = lax.axis_index("wide") * tok_rows
    shifted = lax.dynamic_slice_in_dim(shift_heads, lax.axis_index("narrow") * heads_here, heads_here) > 0

    doubled = jnp.concatenate([seg_ids[-SHIFT:], seg_ids], 0)
    seg_here = lax.dynamic_slice_in_dim(doubled, first_tok, tok_rows + SHIFT)
    seg_q = seg_here[SHIFT:, None]
    windows = jnp.stack([seg_here[b * SHIFT : (b + 2) * SHIFT] for b in range(blocks)])
    odd = (jnp.arange(blocks) % 2 == 1)[None, :, None]
    reaches = (shifted[:, None, None] != odd) | (jnp.arange(2 * SHIFT) >= SHIFT)[None, None, :]
    seg_k = jnp.where(reaches, windows[None], -1)[:, :, None, :]

    wq = w_qkv.transpose(1, 0, 2)
    wo = w_out.reshape(narrow, 2, local_f // 2, -1)
    return layer(hidden, wq, wo, seg_q, seg_k)


def solution(mesh):
    placed = (
        P(("groups", "wide"), None),
        P("wide", None, "narrow"),
        P(None, "wide"),
        P("groups"),
        P(),
    )
    return jax.shard_map(
        per_device,
        mesh=mesh,
        in_specs=placed,
        out_specs=P(("groups", "wide", "narrow"), None),
        check_vma=False,
    )
```

time: 392 us -> 196 us (0.50)
  waiting for transfers between devices: 348 us -> 0 us
  Pallas kernels: 0 us -> 188 us
  matrix products: 22.3 us -> 0 us
  between operations: 13.2 us -> 0.01 us
    all_gather x2 -> x0, waiting for transfers between devices: 251 us -> none  [the longest x1 219 us: per_device(): lax.all_gather(w_qkv, 'wide', axis=0, tiled=True)]
    pallas_call x0 -> x1, Pallas kernels: none -> 188 us  [layer(): pl.pallas_call(functools.partial(layer_kernel, n, narrow, chunks, wo_chun...]
    ppermute x2 -> x0, waiting for transfers between devices: 53.4 us -> none  [from_behind(): return lax.ppermute(block, axis, route)]
    reduce_scatter x1 -> x0, waiting for transfers between devices: 43.3 us -> none  [per_device(): lax.psum_scatter(partial_value.astype(jnp.bfloat16), 'narrow', scatter_di...]
    dot_general x3 -> x0, matrix products: 20 us -> none  [the longest x1 10.9 us: per_device(): jnp.einsum('tr,rcf->tcf', hidden, lax.all_gather(w_qkv, 'wide', axis=0, t...]
  transfers between devices with their start and end apart: 5 -> 0, of which waited for: 4 -> 0; matrix products, arithmetic and copies ran while one was open for 5% -> 0% of each run, Pallas kernels for 0% -> 0%
where the time goes in v2:
time: 196 us; the launch traced here: 194 us
  Pallas kernels  188 us (96%)
  local copies, waits for them, and re-layouts  3.84 us (2%)
  other arithmetic  2.29 us (1%)
    pallas_call x1, Pallas kernels, layer(): pl.pallas_call(functools.partial(layer_kernel, n, narrow, chunks, wo_chun...  188 us

profile of v2, /device:TPU:0, one launch (start us, length us, event | category | flops | bytes accessed | tf_op | source)
XLA Modules:
  0.0 194.4 jit_solution(8776689034769543913)
XLA Ops:
  0.0 0.7 dynamic-slice_compare_fusion
  0.7 0.1 broadcast_compare_fusion
  0.8 0.7 slice.10
  1.5 0.8 fusion
  2.3 0.7 or_select_fusion.segk_ref
  3.0 0.9 copy.6.segq_ref
  3.8 188.2 %shard_map.55 = bf16[128,4096]{1,0:T(8,128)(2,1)} custom-call(bf16[512,4096]{1,0:T(8,128)(2,1)} %hidden_ref.1, bf16[3,1024,512]{2,1,0:T(8,128)(2,1)} %bitcast.6, bf16[4,2,256,1024]{3,2,1,0:T(8,128)(2,1)} %bitcast.5, s32[512,1]{1,0:T(8,128)} %copy.6.segq_ref, s32[4,2,1,512]{3,2,1,0:T(1,128)} %or_select_fusion.segk_ref), custom_call_target="tpu_custom_call" | custom-call | tf_op jit(solution)/shard_map/pallas_call | solution.py:373
  192.1 2.3 %copy.8 = bf16[128,4096]{1,0:T(8,128)(2,1)} copy(bf16[128,4096]{1,0:T(8,128)(2,1)} %shard_map.55) | data formatting | bytes 2097152
  (4 shorter events, 0.0 us)

commit v3 on v2

v3 whole, which is shorter than its diff:
```python
import functools
import math

import jax
import jax.numpy as jnp
from jax import lax
from jax.experimental import pallas as pl
from jax.experimental.pallas import tpu as pltpu
from jax.sharding import PartitionSpec as P

HEAD_DIM = 128
GROUP = 512
SHIFT = 256

masked_out = -1e30
MESH = pl.DeviceIdType.MESH
ROWS = 256
WO_CHUNKS = 4
NEXT_EARLY = 1


def layer_kernel(
    n, narrow, chunks, wo_chunks,
    hidden_ref, wq_ref, wo_ref, segq_ref, segk_ref, out_ref,
    wbuf, acc, wo_buf, q_buf, kv_buf, att, part, pair_in, pair_sum, far_in,
    lent, help_out, help_in,
    own_sem, own_wo,
    qs_r, qs_l, qr, qs_y, qr_y,
    os_r, os_l, o_r, os_y, or_y,
    kv_sem, pair_s, pair_r, far_s, far_r,
    lend_sem, share_s, share_r, help_s, help_r,
):
    me = lax.axis_index("wide")
    y = lax.axis_index("groups")
    spot = lax.axis_index("narrow")
    other = 1 - y
    across_n = narrow // 2
    high, low = spot // 2, lax.rem(spot, 2)
    depth = wq_ref.shape[1]
    heads = wbuf.shape[0]
    phases = heads // 2
    tok = hidden_ref.shape[0]
    share = tok // narrow
    rows = depth // chunks
    steps = (n - 2) * chunks
    wo_rows = wo_buf.shape[2] // wo_chunks
    cols = wo_buf.shape[3]
    blocks = tok // SHIFT
    has_left, has_right = me > 0, me < n - 1
    first, last = me == 0, me == n - 1
    helps_left, helps_right = me == 1, me == n - 2
    helps = jnp.logical_or(helps_left, helps_right)
    right, left = {"wide": me + 1}, {"wide": me - 1}
    after, before = {"wide": lax.rem(me + 1, n)}, {"wide": lax.rem(me + n - 1, n)}
    opposite = {"groups": other}
    pair = {"narrow": high * 2 + 1 - low}
    others = [{"narrow": lax.rem(spot + d, narrow)} for d in range(1, narrow)]
    far = [{"narrow": lax.rem(high + d, across_n) * 2 + low} for d in range(1, across_n)]
    far_from = [{"narrow": lax.rem(high + across_n - d, across_n) * 2 + low} for d in range(1, across_n)]

    barrier = pltpu.get_barrier_semaphore()
    greeted = [after, before, opposite] + others
    for device in greeted:
        pl.semaphore_signal(barrier, inc=1, device_id=device, device_id_type=MESH)

    def w_at(shard, head, c):
        start = pl.multiple_of(shard * depth + c * rows, rows)
        return wbuf.at[head, pl.ds(start, rows)]

    def o_at(shard, part_of, c):
        return wo_buf.at[shard, part_of, pl.ds(pl.multiple_of(c * wo_rows, wo_rows), wo_rows)]

    def wo_own(c):
        return wo_ref.at[spot, y, pl.ds(pl.multiple_of(c * wo_rows, wo_rows), wo_rows)]

    def remote(src, dst, send, recv, device):
        return pltpu.make_async_remote_copy(
            src_ref=src, dst_ref=dst, send_sem=send, recv_sem=recv,
            device_id=device, device_id_type=MESH,
        )

    def q_right(shard, p, c):
        ref = w_at(shard, y * phases + p, c)
        return remote(ref, ref, qs_r.at[p, shard, c], qr.at[p, shard, c], right)

    def q_left(shard, p, c):
        ref = w_at(shard, y * phases + p, c)
        return remote(ref, ref, qs_l.at[p, shard, c], qr.at[p, shard, c], left)

    def q_across(shard, p, c, part_of):
        ref = w_at(shard, part_of * phases + p, c)
        return remote(ref, ref, qs_y.at[p, shard, c], qr_y.at[p, shard, c], opposite)

    def to_right(shard):
        return jnp.logical_and(has_right, jnp.logical_or(jnp.logical_not(helps_right), shard == me))

    def to_left(shard):
        return jnp.logical_and(has_left, jnp.logical_or(jnp.logical_not(helps_left), shard == me))

    def comes_right(s):
        return jnp.logical_and(me - 1 - s >= 0, jnp.logical_or(jnp.logical_not(last), s == 0))

    def comes_left(s):
        return jnp.logical_and(me + 1 + s <= n - 1, jnp.logical_or(jnp.logical_not(first), s == 0))

    def o_right(shard, c, src=None):
        dst = o_at(shard, y, c)
        return remote(dst if src is None else src, dst, os_r.at[shard, c], o_r.at[shard, c], right)

    def o_left(shard, c, src=None):
        dst = o_at(shard, y, c)
        return remote(dst if src is None else src, dst, os_l.at[shard, c], o_r.at[shard, c], left)

    def o_across(shard, c, part_of):
        ref = o_at(shard, part_of, c)
        return remote(ref, ref, os_y.at[shard, c], or_y.at[shard, c], opposite)

    def own_copy(head, i):
        return pltpu.make_async_copy(
            wq_ref.at[i, :, pl.ds(pl.multiple_of(head * HEAD_DIM, HEAD_DIM), HEAD_DIM)],
            wbuf.at[head, pl.ds(pl.multiple_of(me * depth, depth), depth), pl.ds(i * HEAD_DIM, HEAD_DIM)],
            own_sem.at[head, i],
        )

    order = [part_of * phases + p for p in range(phases) for part_of in (y, other)]
    for head in order:
        for i in range(3):
            own_copy(head, i).start()
    own_wo_copy = pltpu.make_async_copy(wo_ref.at[spot], wo_buf.at[me], own_wo)
    own_wo_copy.start()
    pl.semaphore_wait(barrier, len(greeted))

    far_cols = (n - 2) * depth
    my_rows = pl.ds(pl.multiple_of(spot * share, share), share)

    def lend(start, device):
        return remote(
            hidden_ref.at[my_rows, pl.ds(start, far_cols)], lent.at[my_rows],
            lend_sem.at[0], lend_sem.at[1], device,
        )

    @pl.when(first)
    def _():
        lend(2 * depth, right).start()

    @pl.when(last)
    def _():
        lend(0, left).start()

    def send_own(p):
        @pl.loop(0, chunks)
        def _(c):
            @pl.when(has_right)
            def _():
                q_right(me, p, c).start()

            @pl.when(has_left)
            def _():
                q_left(me, p, c).start()

    def send_own_wo():
        @pl.loop(0, wo_chunks)
        def _(c):
            @pl.when(has_right)
            def _():
                o_right(me, c, wo_own(c)).start()

            @pl.when(has_left)
            def _():
                o_left(me, c, wo_own(c)).start()

    def shared(d):
        return remote(
            lent.at[my_rows], lent.at[my_rows], share_s.at[d - 1], share_r.at[d - 1], others[d - 1]
        )

    def add(shard, head, c):
        start = pl.multiple_of(shard * depth + c * rows, rows)
        acc[head] += jnp.dot(
            hidden_ref[:, pl.ds(start, rows)], wbuf[head, pl.ds(start, rows)],
            preferred_element_type=jnp.float32,
        )

    def add_across(p, t):
        s, c = t // chunks, lax.rem(t, chunks)
        for there, shard in ((comes_right(s), me - 1 - s), (comes_left(s), me + 1 + s)):
            @pl.when(there)
            def _():
                q_across(shard, p, c, other).wait_recv()
                add(shard, other * phases + p, c)

    def help_copy(p, device):
        return remote(help_out.at[p], help_in.at[p], help_s.at[p], help_r.at[p], device)

    acc[...] = jnp.zeros_like(acc)
    for p in range(phases):
        if p == 0:
            for i in range(3):
                own_copy(order[0], i).wait()
            send_own(0)

            @pl.when(helps)
            def _():
                lend(0, left).wait_recv()
                for d in range(1, narrow):
                    shared(d).start()

            for head in order[1:]:
                for i in range(3):
                    own_copy(head, i).wait()

        @pl.loop(0, 2 * chunks)
        def _(i):
            add(me, i // chunks * phases + p, lax.rem(i, chunks))

        @pl.loop(0, steps)
        def _(t):
            s, c = t // chunks, lax.rem(t, chunks)

            @pl.when(comes_right(s))
            def _():
                q_right(me - 1 - s, p, c).wait_recv()

                @pl.when(to_right(me - 1 - s))
                def _():
                    q_right(me - 1 - s, p, c).start()

                q_across(me - 1 - s, p, c, y).start()

            @pl.when(comes_left(s))
            def _():
                q_left(me + 1 + s, p, c).wait_recv()

                @pl.when(to_left(me + 1 + s))
                def _():
                    q_left(me + 1 + s, p, c).start()

                q_across(me + 1 + s, p, c, y).start()

            @pl.when(t == steps - 2 * NEXT_EARLY)
            def _():
                if p + 1 < phases:
                    send_own(p + 1)

            for there, shard in ((comes_right(s), me - 1 - s), (comes_left(s), me + 1 + s)):
                @pl.when(there)
                def _():
                    add(shard, y * phases + p, c)

            @pl.when(t > 0)
            def _():
                add_across(p, t - 1)

        add_across(p, steps - 1)

        @pl.when(helps)
        def _():
            if p == 0:
                for d in range(1, narrow):
                    from_rows = pl.ds(pl.multiple_of(lax.rem(spot + narrow - d, narrow) * share, share), share)
                    remote(
                        lent.at[my_rows], lent.at[from_rows], share_s.at[d - 1], share_r.at[d - 1], others[d - 1]
                    ).wait_recv()
            start = pl.multiple_of(jnp.where(helps_left, 2 * depth, 0), depth)
            for part_of in range(2):
                help_out[p, part_of] = jnp.dot(
                    lent[...], wbuf[part_of * phases + p, pl.ds(start, far_cols)],
                    preferred_element_type=jnp.float32,
                ).astype(jnp.bfloat16)

        @pl.when(helps_left)
        def _():
            help_copy(p, left).start()

        @pl.when(helps_right)
        def _():
            help_copy(p, right).start()

    send_own_wo()
    for p in range(phases):
        @pl.when(jnp.logical_or(first, last))
        def _():
            help_copy(p, left).wait_recv()
            for part_of in range(2):
                acc[part_of * phases + p] += help_in[p, part_of].astype(jnp.float32)

    for h in range(heads):
        q_buf[h] = acc[h, :, :HEAD_DIM].astype(jnp.bfloat16)
        kv_buf[h, SHIFT:] = acc[h, :, HEAD_DIM:].astype(jnp.bfloat16)

    kv_copy = remote(
        kv_buf.at[:, pl.ds(tok, SHIFT)], kv_buf.at[:, pl.ds(0, SHIFT)],
        kv_sem.at[0], kv_sem.at[1], after,
    )
    kv_copy.start()

    causal = lax.broadcasted_iota(jnp.int32, (SHIFT, 2 * SHIFT), 1) <= (
        lax.broadcasted_iota(jnp.int32, (SHIFT, 2 * SHIFT), 0) + SHIFT
    )

    def attend(h, b):
        mine, seen = slice(b * SHIFT, (b + 1) * SHIFT), slice(b * SHIFT, (b + 2) * SHIFT)
        scores = lax.dot_general(
            q_buf[h, mine], kv_buf[h, seen, :HEAD_DIM], (((1,), (1,)), ((), ())),
            preferred_element_type=jnp.float32,
        ) * (1.0 / math.sqrt(HEAD_DIM))
        allowed = causal & (segq_ref[mine, :] == segk_ref[h, b])
        scores = jnp.where(allowed, scores, masked_out)
        exponent = jnp.exp(scores - jnp.max(scores, axis=-1, keepdims=True))
        weights = exponent / jnp.sum(exponent, axis=-1, keepdims=True)
        att[mine, h * HEAD_DIM : (h + 1) * HEAD_DIM] = jnp.dot(
            weights.astype(jnp.bfloat16), kv_buf[h, seen, HEAD_DIM:], preferred_element_type=jnp.float32
        ).astype(jnp.bfloat16)

    least = jnp.minimum(me, n - 1 - me)

    def block_of(k):
        turn = (k + 1) // 2
        near = jnp.where(lax.rem(k, 2) == 1, me - turn, me + turn)
        rest = jnp.where(me > least, me - (k - least), me + (k - least))
        return jnp.where(k <= 2 * least, near, rest)

    def pass_on(k):
        shard = block_of(k)

        @pl.loop(0, wo_chunks)
        def _(c):
            o_right(shard, c).wait_recv()

            @pl.when(jnp.logical_and(shard < me, has_right))
            def _():
                o_right(shard, c).start()

            @pl.when(jnp.logical_and(shard > me, has_left))
            def _():
                o_left(shard, c).start()

            o_across(shard, c, y).start()

    def pair_copy(shard, a):
        return remote(
            part.at[shard, a * 2 + 1 - low], pair_in.at[shard, a],
            pair_s.at[shard, a], pair_r.at[shard, a], pair,
        )

    def far_copy(shard, d):
        a = lax.rem(high + d, across_n)
        return remote(
            pair_sum.at[shard, a], far_in.at[shard, d - 1],
            far_s.at[shard, d - 1], far_r.at[shard, d - 1], far[d - 1],
        )

    def far_arrival(shard, d):
        return remote(
            pair_sum.at[shard, high], far_in.at[shard, d - 1],
            far_s.at[shard, d - 1], far_r.at[shard, d - 1], far_from[d - 1],
        )

    def multiply(k):
        shard = block_of(k)
        width = att.shape[1] // 2
        for p in range(narrow):
            a_rows = att[p * share : (p + 1) * share, :]
            total = jnp.dot(a_rows[:, :width], wo_buf[shard, 0], preferred_element_type=jnp.float32)
            total += jnp.dot(a_rows[:, width:], wo_buf[shard, 1], preferred_element_type=jnp.float32)
            part[shard, p] = total.astype(jnp.bfloat16)
        for a in range(across_n):
            pair_copy(shard, a).start()

    def sum_pair(k):
        shard = block_of(k)
        for a in range(across_n):
            pair_copy(shard, a).wait_recv()
            total = part[shard, a * 2 + low].astype(jnp.float32) + pair_in[shard, a].astype(jnp.float32)
            pair_sum[shard, a] = total.astype(jnp.bfloat16)
        for d in range(1, across_n):
            far_copy(shard, d).start()

    def finish(k):
        shard = block_of(k)
        total = part[shard, high * 2 + low].astype(jnp.float32) + pair_in[shard, high].astype(jnp.float32)
        for d in range(1, across_n):
            far_arrival(shard, d).wait_recv()
            total += far_in[shard, d - 1].astype(jnp.float32)
        out_ref[:, pl.ds(pl.multiple_of(shard * cols, cols), cols)] = total.astype(out_ref.dtype)

    for b in range(1, blocks):
        for h in range(heads):
            attend(h, b)
    pass_on(1)
    pass_on(2)
    kv_copy.wait_recv()
    for h in range(heads):
        attend(h, 0)
    own_wo_copy.wait()
    multiply(0)

    @pl.loop(1, n)
    def _(k):
        @pl.when(k > 2)
        def _():
            pass_on(k)

        sum_pair(k - 1)

        @pl.when(k > 1)
        def _():
            finish(k - 2)

        shard = block_of(k)

        @pl.loop(0, wo_chunks)
        def _(c):
            o_across(shard, c, other).wait_recv()

        multiply(k)

    sum_pair(n - 1)
    finish(n - 2)
    finish(n - 1)

    kv_copy.wait_send()

    @pl.loop(0, n)
    def _(shard):
        for a in range(across_n):
            pair_copy(shard, a).wait_send()
        for d in range(1, across_n):
            far_copy(shard, d).wait_send()
        @pl.loop(0, chunks)
        def _(c):
            for p in range(phases):
                @pl.when(jnp.logical_and(shard <= me, to_right(shard)))
                def _():
                    q_right(shard, p, c).wait_send()

                @pl.when(jnp.logical_and(shard >= me, to_left(shard)))
                def _():
                    q_left(shard, p, c).wait_send()

                came = jnp.where(shard < me, comes_right(me - 1 - shard), comes_left(shard - me - 1))

                @pl.when(jnp.logical_and(shard != me, came))
                def _():
                    q_across(shard, p, c, y).wait_send()

        @pl.loop(0, wo_chunks)
        def _(c):
            @pl.when(jnp.logical_and(shard <= me, has_right))
            def _():
                o_right(shard, c).wait_send()

            @pl.when(jnp.logical_and(shard >= me, has_left))
            def _():
                o_left(shard, c).wait_send()

            @pl.when(shard != me)
            def _():
                o_across(shard, c, y).wait_send()

    @pl.when(jnp.logical_or(first, last))
    def _():
        lend(0, left).wait_send()

    @pl.when(helps)
    def _():
        for d in range(1, narrow):
            shared(d).wait_send()
        for p in range(phases):
            help_copy(p, left).wait_send()


def layer(hidden, wq, wo, seg_q, seg_k):
    n, narrow = lax.axis_size("wide"), lax.axis_size("narrow")
    tok, width = hidden.shape
    depth = wq.shape[1]
    heads = wq.shape[2] // HEAD_DIM
    phases = heads // 2
    chunks = max(1, depth // ROWS)
    wo_chunks = WO_CHUNKS
    cols = wo.shape[3]
    share = tok // narrow
    vmem = pl.BlockSpec(memory_space=pltpu.VMEM)
    hbm = pl.BlockSpec(memory_space=pl.ANY)
    dma = pltpu.SemaphoreType.DMA
    bf16 = jnp.bfloat16
    return pl.pallas_call(
        functools.partial(layer_kernel, n, narrow, chunks, wo_chunks),
        out_shape=jax.ShapeDtypeStruct((share, n * cols), bf16),
        in_specs=[vmem, hbm, hbm, vmem, vmem],
        out_specs=vmem,
        scratch_shapes=[
            pltpu.VMEM((heads, width, 3 * HEAD_DIM), bf16),
            pltpu.VMEM((heads, tok, 3 * HEAD_DIM), jnp.float32),
            pltpu.VMEM((n,) + wo.shape[1:], bf16),
            pltpu.VMEM((heads, tok, HEAD_DIM), bf16),
            pltpu.VMEM((heads, tok + SHIFT, 2 * HEAD_DIM), bf16),
            pltpu.VMEM((tok, heads * HEAD_DIM), bf16),
            pltpu.VMEM((n, narrow, share, cols), bf16),
            pltpu.VMEM((n, narrow // 2, share, cols), bf16),
            pltpu.VMEM((n, narrow // 2, share, cols), bf16),
            pltpu.VMEM((n, max(1, narrow // 2 - 1), share, cols), bf16),
            pltpu.VMEM((tok, (n - 2) * depth), bf16),
            pltpu.VMEM((phases, 2, tok, 3 * HEAD_DIM), bf16),
            pltpu.VMEM((phases, 2, tok, 3 * HEAD_DIM), bf16),
            dma((heads, 3)),
            dma(()),
        ]
        + [dma((phases, n, chunks))] * 5
        + [dma((n, wo_chunks))] * 5
        + [dma((2,))]
        + [dma((n, narrow // 2))] * 2
        + [dma((n, max(1, narrow // 2 - 1)))] * 2
        + [dma((2,))]
        + [dma((narrow - 1,))] * 2
        + [dma((phases,))] * 2,
        compiler_params=pltpu.CompilerParams(
            collective_id=0, has_side_effects=True, vmem_limit_bytes=58 * 1024 * 1024
        ),
    )(hidden, wq, wo, seg_q, seg_k)


def per_device(hidden, w_qkv, w_out, seg_ids, shift_heads):
    tok_rows = hidden.shape[0]
    local_f = w_qkv.shape[2]
    heads_here = local_f // HEAD_DIM
    blocks = tok_rows // SHIFT
    narrow = lax.axis_size("narrow")
    first_tok = lax.axis_index("wide") * tok_rows
    shifted = lax.dynamic_slice_in_dim(shift_heads, lax.axis_index("narrow") * heads_here, heads_here) > 0

    doubled = jnp.concatenate([seg_ids[-SHIFT:], seg_ids], 0)
    seg_here = lax.dynamic_slice_in_dim(doubled, first_tok, tok_rows + SHIFT)
    seg_q = seg_here[SHIFT:, None]
    windows = jnp.stack([seg_here[b * SHIFT : (b + 2) * SHIFT] for b in range(blocks)])
    odd = (jnp.arange(blocks) % 2 == 1)[None, :, None]
    reaches = (shifted[:, None, None] != odd) | (jnp.arange(2 * SHIFT) >= SHIFT)[None, None, :]
    seg_k = jnp.where(reaches, windows[None], -1)[:, :, None, :]

    wq = w_qkv.transpose(1, 0, 2)
    wo = w_out.reshape(narrow, 2, local_f // 2, -1)
    return layer(hidden, wq, wo, seg_q, seg_k)


def solution(mesh):
    placed = (
        P(("groups", "wide"), None),
        P("wide", None, "narrow"),
        P(None, "wide"),
        P("groups"),
        P(),
    )
    return jax.shard_map(
        per_device,
        mesh=mesh,
        in_specs=placed,
        out_specs=P(("groups", "wide", "narrow"), None),
        check_vma=False,
    )
```

time: 196 us -> 227 us (1.16)
  Pallas kernels: 188 us -> 220 us
    pallas_call x1, Pallas kernels: 188 us -> 220 us  [layer(): pl.pallas_call(functools.partial(layer_kernel, n, narrow, chunks, wo_chun...]
where the time goes in v3:
time: 227 us; the launch traced here: 226 us
  Pallas kernels  220 us (97%)
  local copies, waits for them, and re-layouts  3.84 us (2%)
  other arithmetic  2.29 us (1%)
    pallas_call x1, Pallas kernels, layer(): pl.pallas_call(functools.partial(layer_kernel, n, narrow, chunks, wo_chun...  220 us

profile of v3, /device:TPU:0, one launch (start us, length us, event | category | flops | bytes accessed | tf_op | source)
XLA Modules:
  0.0 226.0 jit_solution(15547008605935778319)
XLA Ops:
  0.0 0.7 dynamic-slice_compare_fusion
  0.7 0.1 broadcast_compare_fusion
  0.8 0.7 slice.10
  1.5 0.8 fusion
  2.3 0.7 or_select_fusion.segk_ref
  3.0 0.9 copy.6.segq_ref
  3.8 219.8 %shard_map.55 = bf16[128,4096]{1,0:T(8,128)(2,1)} custom-call(bf16[512,4096]{1,0:T(8,128)(2,1)} %hidden_ref.1, bf16[3,1024,512]{2,1,0:T(8,128)(2,1)} %bitcast.6, bf16[4,2,256,1024]{3,2,1,0:T(8,128)(2,1)} %bitcast.5, s32[512,1]{1,0:T(8,128)} %copy.6.segq_ref, s32[4,2,1,512]{3,2,1,0:T(1,128)} %or_select_fusion.segk_ref), custom_call_target="tpu_custom_call" | custom-call | tf_op jit(solution)/shard_map/pallas_call | solution.py:487
  223.7 2.3 %copy.8 = bf16[128,4096]{1,0:T(8,128)(2,1)} copy(bf16[128,4096]{1,0:T(8,128)(2,1)} %shard_map.55) | data formatting | bytes 2097152
  (4 shorter events, 0.0 us)

commit v4 on v2

--- a/solution.py
+++ b/solution.py
@@ -15,7 +15,7 @@
 masked_out = -1e30
 MESH = pl.DeviceIdType.MESH
 ROWS = 128
-WO_CHUNKS = 2
+WO_CHUNKS = 4
 
 
 def layer_kernel(
@@ -147,9 +147,24 @@
                 q_across(shard, c, other).wait_recv()
                 add(shard, other, c)
 
+    def send_own_wo():
+        @pl.loop(0, wo_chunks)
+        def _(c):
+            @pl.when(has_right)
+            def _():
+                o_right(me, c, wo_own(c)).start()
+
+            @pl.when(has_left)
+            def _():
+                o_left(me, c, wo_own(c)).start()
+
     @pl.loop(0, steps)
     def _(t):
         s, c = t // chunks, lax.rem(t, chunks)
+
+        @pl.when(t == steps - chunks)
+        def _():
+            send_own_wo()
 
         @pl.when(me - 1 - s >= 0)
         def _():
@@ -191,16 +206,6 @@
         kv_sem.at[0], kv_sem.at[1], after,
     )
     kv_copy.start()
-
-    @pl.loop(0, wo_chunks)
-    def _(c):
-        @pl.when(has_right)
-        def _():
-            o_right(me, c, wo_own(c)).start()
-
-        @pl.when(has_left)
-        def _():
-            o_left(me, c, wo_own(c)).start()
 
     causal = lax.broadcasted_iota(jnp.int32, (SHIFT, 2 * SHIFT), 1) <= (
         lax.broadcasted_iota(jnp.int32, (SHIFT, 2 * SHIFT), 0) + SHIFT
@@ -300,6 +305,7 @@
         for h in range(heads):
             attend(h, b)
     pass_on(1)
+    pass_on(2)
     kv_copy.wait_recv()
     for h in range(heads):
         attend(h, 0)
@@ -308,7 +314,7 @@
 
     @pl.loop(1, n)
     def _(k):
-        @pl.when(k > 1)
+        @pl.when(k > 2)
         def _():
             pass_on(k)
 

time: 196 us -> 190 us (0.969)
  Pallas kernels: 188 us -> 183 us
    pallas_call x1, Pallas kernels: 188 us -> 183 us  [layer(): pl.pallas_call(functools.partial(layer_kernel, n, narrow, chunks, wo_chun...]
where the time goes in v4:
time: 190 us
  Pallas kernels  183 us (96%)
  local copies, waits for them, and re-layouts  3.84 us (2%)
  other arithmetic  2.29 us (1%)
    pallas_call x1, Pallas kernels, layer(): pl.pallas_call(functools.partial(layer_kernel, n, narrow, chunks, wo_chun...  183 us

profile of v4, /device:TPU:0, one launch (start us, length us, event | category | flops | bytes accessed | tf_op | source)
XLA Modules:
  0.0 189.5 jit_solution(9049819380262095379)
XLA Ops:
  0.0 0.7 dynamic-slice_compare_fusion
  0.7 0.1 broadcast_compare_fusion
  0.8 0.7 slice.10
  1.5 0.8 fusion
  2.3 0.7 or_select_fusion.segk_ref
  3.0 0.9 copy.6.segq_ref
  3.8 183.4 %shard_map.55 = bf16[128,4096]{1,0:T(8,128)(2,1)} custom-call(bf16[512,4096]{1,0:T(8,128)(2,1)} %hidden_ref.1, bf16[3,1024,512]{2,1,0:T(8,128)(2,1)} %bitcast.6, bf16[4,2,256,1024]{3,2,1,0:T(8,128)(2,1)} %bitcast.5, s32[512,1]{1,0:T(8,128)} %copy.6.segq_ref, s32[4,2,1,512]{3,2,1,0:T(1,128)} %or_select_fusion.segk_ref), custom_call_target="tpu_custom_call" | custom-call | tf_op jit(solution)/shard_map/pallas_call | solution.py:379
  187.2 2.3 %copy.8 = bf16[128,4096]{1,0:T(8,128)(2,1)} copy(bf16[128,4096]{1,0:T(8,128)(2,1)} %shard_map.55) | data formatting | bytes 2097152
  (4 shorter events, 0.0 us)
